TPU v7x, 256 devices: a whole 4x4x8 slice. The times are simulated.
256 devices in a mesh: seq: 16 (over z, core), head: 16 (over x, y).
Axes of the slice: x: 4, y: 4, z: 8, core: 2. Of those that a mesh axis runs over, the one named last changes fastest.
Arguments:
- x_in: bfloat16 [16384, 8192], P('seq', 'head'), may hold values from -6 to 6
- z_gate: bfloat16 [16384, 8192], P('seq', 'head'), may hold values from -6 to 6
- b_in: bfloat16 [16384, 128], P('seq'), may hold values from -6.5 to 6.5
- c_in: bfloat16 [16384, 128], P('seq'), may hold values from -6 to 6
- dt_raw: float32 [16384, 128], P('seq', 'head'), may hold values from -7.5 to 263.144
- a_log: float32 [128], P('head'), may hold values from -12 to 3.5, as said below
- d_skip: float32 [128], P('head'), may hold values from 0.5 to 1.5
- conv_x: float32 [4, 8192], P(None, 'head'), may hold values from -3 to 3
- conv_bc: float32 [4, 256], replicated, may hold values from -0.8 to 0.8
- norm_gain: float32 [8192], P('head'), may hold values from 0.1 to 1.9
- w_out: bfloat16 [8192, 4096], P('head'), may hold values from -0.0625 to 0.0625
Outputs:
- mixed: bfloat16 [16384, 4096], P(('seq', 'head'))
Inputs may be any that keep to these rules, and one draw needn't show every extreme that they name: `a_log`: logarithm of each head's decay rate.
All inputs are finite; a program needn't handle non-finite values.
Results may differ from a plain program's by a relative error of at most 0.018.
Values may be sent and summed in bfloat16 or wider, within the bound.
No kernel may reach another device: no remote copies, remote signals or barrier semaphores. Data moves between devices by JAX's collectives and lax.ppermute only.
A program may use at most 64 MiB of HBM per device.

v0:
```python
import jax
import jax.numpy as jnp
from jax import lax
from jax.sharding import PartitionSpec as P

HEAD_DIM = 64
SPAN = 256
INNER = 8192
norm_eps = 1e-05


def passed_along(block, axis, distance):
    devices = range(lax.axis_size(axis))
    route = [(i - distance, i) for i in devices if i - distance in devices]
    return lax.ppermute(block, axis, route)


def carried_in(x, axis, combine, identity):
    devices, here = (lax.axis_size(axis), lax.axis_index(axis))
    everything = jax.tree.map(
        lambda part, kind: lax.all_gather(part.astype(kind), axis), x, (jnp.bfloat16, jnp.bfloat16)
    )
    start = jax.tree.map(
        lambda part, zero: jnp.broadcast_to(jnp.asarray(zero, part.dtype), part.shape), x, identity
    )

    def turn(k, before):
        reached = k < here
        new = combine(
            before, jax.tree.map(lambda part, own: part[k].astype(own.dtype), everything, x)
        )
        return jax.tree.map(lambda a, b: jnp.where(reached, a, b), new, before)

    return lax.fori_loop(0, devices, turn, start)


def causal_conv(values, rim, weight):
    n_rows = values.shape[0]
    padded = jnp.concatenate([rim.astype(jnp.float32), values.astype(jnp.float32)], axis=0)
    result = weight[0][None, :] * padded[0:n_rows]
    for offset in range(1, weight.shape[0]):
        result = result + weight[offset][None, :] * padded[offset : offset + n_rows]
    return jax.nn.silu(result).astype(jnp.bfloat16)


def span_step(memory, pieces):
    x_part, b_part, c_part, step_part, decay_part = pieces
    running = jnp.cumsum(decay_part, axis=0)
    length = x_part.shape[0]
    positions = lax.iota(jnp.int32, length)
    causal = positions[:, None] >= positions[None, :]
    spread = jnp.where(causal[:, :, None], running[:, None, :] - running[None, :, :], -1e30)
    scores = jnp.dot(c_part, b_part.T, preferred_element_type=jnp.float32)
    b_wide = b_part.astype(jnp.float32)
    c_wide = c_part.astype(jnp.float32)
    mixing = jnp.exp(spread) * scores[:, :, None] * step_part[None, :, :]
    inside = jnp.einsum("ijh,jhp->ihp", mixing, x_part, precision=lax.Precision.HIGHEST)
    earlier = (
        jnp.einsum("in,hpn->ihp", c_wide, memory, precision=lax.Precision.HIGHEST)
        * jnp.exp(running)[:, :, None]
    )
    final_decay = running[length - 1]
    weights = jnp.exp(final_decay[None, :] - running) * step_part
    update = jnp.einsum(
        "jhp,jn->hpn", x_part * weights[:, :, None], b_wide, precision=lax.Precision.HIGHEST
    )
    new_memory = memory * jnp.exp(final_decay)[:, None, None] + update
    return (new_memory, inside + earlier)


def local(x_in, z_gate, b_in, c_in, dt_raw, a_log, d_skip, conv_x, conv_bc, norm_gain, w_out):
    n_rows = x_in.shape[0]
    rim_rows = conv_x.shape[0] - 1
    state_size = b_in.shape[1]
    head_count = dt_raw.shape[1]
    bc_in = jnp.concatenate([b_in, c_in], axis=1)
    x_rim, bc_rim = passed_along((x_in[n_rows - rim_rows :], bc_in[n_rows - rim_rows :]), "seq", 1)
    x_conv = causal_conv(x_in, x_rim, conv_x)
    bc_conv = causal_conv(bc_in, bc_rim, conv_bc)
    b_conv = bc_conv[:, :state_size]
    c_conv = bc_conv[:, state_size:]
    dt_step = jax.nn.softplus(dt_raw)
    log_decay = -jnp.exp(a_log)[None, :] * dt_step
    x_heads = x_conv.astype(jnp.float32).reshape(n_rows, head_count, HEAD_DIM)
    blocks = n_rows // SPAN

    def split_blocks(values):
        return values.reshape((blocks, SPAN) + values.shape[1:])

    start = jnp.zeros((head_count, HEAD_DIM, state_size), jnp.float32)
    final_state, outputs = lax.scan(
        span_step,
        start,
        (
            split_blocks(x_heads),
            split_blocks(b_conv),
            split_blocks(c_conv),
            split_blocks(dt_step),
            split_blocks(log_decay),
        ),
    )
    total_decay = jnp.sum(log_decay, axis=0)

    def combine(earlier, later):
        return (earlier[0] + later[0], jnp.exp(later[0])[:, None, None] * earlier[1] + later[1])

    identity = (jnp.zeros_like(total_decay), jnp.zeros_like(final_state))
    _, incoming = carried_in((total_decay, final_state), "seq", combine, identity)
    inside_segment = jnp.cumsum(log_decay, axis=0)
    carried = (
        jnp.einsum(
            "ln,hpn->lhp", c_conv.astype(jnp.float32), incoming, precision=lax.Precision.HIGHEST
        )
        * jnp.exp(inside_segment)[:, :, None]
    )
    ssd = outputs.reshape(n_rows, head_count, HEAD_DIM) + carried + d_skip[None, :, None] * x_heads
    gated = ssd.reshape(n_rows, head_count * HEAD_DIM) * jax.nn.silu(z_gate.astype(jnp.float32))
    squares = lax.psum(jnp.sum(gated * gated, axis=1), "head")
    normed = (gated * lax.rsqrt(squares / INNER + norm_eps)[:, None] * norm_gain[None, :]).astype(
        jnp.bfloat16
    )
    return lax.psum_scatter(
        jnp.dot(normed, w_out, preferred_element_type=jnp.float32).astype(jnp.bfloat16),
        "head",
        scatter_dimension=0,
        tiled=True,
    )


def solution(mesh):
    in_specs = (
        P("seq", "head"),
        P("seq", "head"),
        P("seq", None),
        P("seq", None),
        P("seq", "head"),
        P("head"),
        P("head"),
        P(None, "head"),
        P(),
        P("head"),
        P("head", None),
    )
    out_specs = P(("seq", "head"), None)
    return jax.shard_map(local, mesh=mesh, in_specs=in_specs, out_specs=out_specs, check_vma=False)
```

profile of v0, /device:TPU:2, one launch (start us, length us, event | category | flops | bytes accessed | tf_op | source)
XLA Modules:
  0.0 321.9 jit_solution(4716732184914080873)
XLA Ops:
  8.7 1.7 collective-permute-start.1
  11.1 4.1 %collective-permute-start = (bf16[3,512]{1,0:T(4,128)(2,1)S(1)}, bf16[3,512]{1,0:T(4,128)(2,1)S(1)}, u32[]{:S(2)}, u32[]{:S(2)}) collective-permute-start(bf16[3,512]{1,0:T(4,128)(2,1)S(1)} %slice.70), channel_id=1, source_target_pairs={{0,16},{16,32},{32,48},{48,64},{64,80},{80,96},{96,112},{112,128},... | collective-permute-start | bytes 9224 | tf_op jit(solution)/shard_map/ppermute | solution.py:15
  23.1 2.4 reshape.114
  25.5 3.8 %copy.35 = f32[4,256,8,64]{1,3,2,0:T(8,128)} copy(f32[4,256,8,64]{3,2,1,0:T(8,128)} %reshape.114) | data formatting | bytes 4194304
  29.3 85.7 %while.27 = (s32[]{:T(128)}, f32[8,64,128]{2,1,0:T(8,128)S(1)}, f32[4,256,8,64]{1,0,3,2:T(4,128)}, f32[4,256,8]{1,2,0:T(8,128)S(1)}, f32[4,256,8,64]{1,3,2,0:T(8...) while((s32[]{:T(128)}, f32[8,64,128]{2,1,0:T(8,128)S(1)}, ...), condition=%wide.region_3.4_spmd.clone, body=%wide.region_0.3_spmd.clone.sunk | while | flops 825167872 | bytes 6557484 | solution.py:91
  31.6 3.5 %fusion.99 = f32[256,8,64]{0,2,1:T(8,128)S(1)} fusion(f32[256,8]{0,1:T(8,128)S(1)} %get-tuple-element.338, f32[256,256]{1,0:T(8,128)S(1)} %fusion.98, f32[256,8]{0,1:T(8,128)S(1)} %get-tuple-element.336, pred[256,256]{1,0:T(8,128)(4,1)S(1)} %iota_compare_fusion.2, f32[4,256,8,64]{1,3,2,0:T(8,128)} %get-tuple-element.371, s32[]{:T(128)} %get-tuple-element.356), kind=kOutput, calls=%fused_computation.12.clone.1 | convolution fusion | flops 404750336 | bytes 1401344 | tf_op jit(solution)/shard_map/while/body/eval_jaxpr/ijh,jhp->ihp/dot_general | solution.py:57
  36.9 12.3 %dynamic_update_slice.6 = f32[4,256,8,64]{1,0,3,2:T(4,128)} dynamic-update-slice(f32[4,256,8,64]{1,0,3,2:T(4,128)} %get-tuple-element.358, f32[1,256,8,64]{1,0,3,2:T(1,128)S(1)} %copy.52, s32[]{:T(128)} %get-tuple-element.356, s32[]{:T(128)} %constant.63.clone.1..sunk, s32[]{:T(128)} %constant.63.clone.1..sunk, s32[]{:T(128)} %constant.63.clone.1..sunk) | dynamic-update-slice | bytes 1048580 | tf_op jit(solution)/shard_map/while/body/jit(dynamic_update_index_in_dim)/dynamic_update_slice | solution.py:91
  53.0 3.5 %fusion.99 = f32[256,8,64]{0,2,1:T(8,128)S(1)} fusion(f32[256,8]{0,1:T(8,128)S(1)} %get-tuple-element.338, f32[256,256]{1,0:T(8,128)S(1)} %fusion.98, f32[256,8]{0,1:T(8,128)S(1)} %get-tuple-element.336, pred[256,256]{1,0:T(8,128)(4,1)S(1)} %iota_compare_fusion.2, f32[4,256,8,64]{1,3,2,0:T(8,128)} %get-tuple-element.371, s32[]{:T(128)} %get-tuple-element.356), kind=kOutput, calls=%fused_computation.12.clone.1 | convolution fusion | flops 404750336 | bytes 1401344 | tf_op jit(solution)/shard_map/while/body/eval_jaxpr/ijh,jhp->ihp/dot_general | solution.py:57
  58.3 12.3 %dynamic_update_slice.6 = f32[4,256,8,64]{1,0,3,2:T(4,128)} dynamic-update-slice(f32[4,256,8,64]{1,0,3,2:T(4,128)} %get-tuple-element.358, f32[1,256,8,64]{1,0,3,2:T(1,128)S(1)} %copy.52, s32[]{:T(128)} %get-tuple-element.356, s32[]{:T(128)} %constant.63.clone.1..sunk, s32[]{:T(128)} %constant.63.clone.1..sunk, s32[]{:T(128)} %constant.63.clone.1..sunk) | dynamic-update-slice | bytes 1048580 | tf_op jit(solution)/shard_map/while/body/jit(dynamic_update_index_in_dim)/dynamic_update_slice | solution.py:91
  74.4 3.5 %fusion.99 = f32[256,8,64]{0,2,1:T(8,128)S(1)} fusion(f32[256,8]{0,1:T(8,128)S(1)} %get-tuple-element.338, f32[256,256]{1,0:T(8,128)S(1)} %fusion.98, f32[256,8]{0,1:T(8,128)S(1)} %get-tuple-element.336, pred[256,256]{1,0:T(8,128)(4,1)S(1)} %iota_compare_fusion.2, f32[4,256,8,64]{1,3,2,0:T(8,128)} %get-tuple-element.371, s32[]{:T(128)} %get-tuple-element.356), kind=kOutput, calls=%fused_computation.12.clone.1 | convolution fusion | flops 404750336 | bytes 1401344 | tf_op jit(solution)/shard_map/while/body/eval_jaxpr/ijh,jhp->ihp/dot_general | solution.py:57
  79.7 12.3 %dynamic_update_slice.6 = f32[4,256,8,64]{1,0,3,2:T(4,128)} dynamic-update-slice(f32[4,256,8,64]{1,0,3,2:T(4,128)} %get-tuple-element.358, f32[1,256,8,64]{1,0,3,2:T(1,128)S(1)} %copy.52, s32[]{:T(128)} %get-tuple-element.356, s32[]{:T(128)} %constant.63.clone.1..sunk, s32[]{:T(128)} %constant.63.clone.1..sunk, s32[]{:T(128)} %constant.63.clone.1..sunk) | dynamic-update-slice | bytes 1048580 | tf_op jit(solution)/shard_map/while/body/jit(dynamic_update_index_in_dim)/dynamic_update_slice | solution.py:91
  95.8 3.5 %fusion.99 = f32[256,8,64]{0,2,1:T(8,128)S(1)} fusion(f32[256,8]{0,1:T(8,128)S(1)} %get-tuple-element.338, f32[256,256]{1,0:T(8,128)S(1)} %fusion.98, f32[256,8]{0,1:T(8,128)S(1)} %get-tuple-element.336, pred[256,256]{1,0:T(8,128)(4,1)S(1)} %iota_compare_fusion.2, f32[4,256,8,64]{1,3,2,0:T(8,128)} %get-tuple-element.371, s32[]{:T(128)} %get-tuple-element.356), kind=kOutput, calls=%fused_computation.12.clone.1 | convolution fusion | flops 404750336 | bytes 1401344 | tf_op jit(solution)/shard_map/while/body/eval_jaxpr/ijh,jhp->ihp/dot_general | solution.py:57
  101.2 12.3 %dynamic_update_slice.6 = f32[4,256,8,64]{1,0,3,2:T(4,128)} dynamic-update-slice(f32[4,256,8,64]{1,0,3,2:T(4,128)} %get-tuple-element.358, f32[1,256,8,64]{1,0,3,2:T(1,128)S(1)} %copy.52, s32[]{:T(128)} %get-tuple-element.356, s32[]{:T(128)} %constant.63.clone.1..sunk, s32[]{:T(128)} %constant.63.clone.1..sunk, s32[]{:T(128)} %constant.63.clone.1..sunk) | dynamic-update-slice | bytes 1048580 | tf_op jit(solution)/shard_map/while/body/jit(dynamic_update_index_in_dim)/dynamic_update_slice | solution.py:91
  117.4 26.1 %all-reduce = bf16[128]{0:T(256)(128)(2,1)S(1)} all-reduce(bf16[128]{0:T(256)(128)(2,1)S(1)} %dynamic-update-slice), channel_id=2, replica_groups=mesh['seq'=16,'head'=16] {'seq'}, use_global_device_ids=true, to_apply=%add | all-reduce | flops 128 | bytes 512
  143.6 2.3 reduce-window.16
  146.3 1.8 copy.38
  148.1 2.4 reshape.95
  150.5 6.7 %all-gather.4.cloned.1.call-done = bf16[128,64,128]{2,1,0:T(8,128)(2,1)} async-done(((bf16[8,64,128]{2,1,0:T(8,128)(2,1)}), bf16[128,64,128]{2,1,0:T(8,128)(2,1)}) %all-gather.4.cloned.1.call-update) | async-done | bytes 2097168 | tf_op jit(solution)/shard_map/all_gather | solution.py:21
  157.2 16.9 %while.28 = (s32[]{:T(128)}, f32[8,64,128]{2,1,0:T(8,128)S(1)}, s32[]{:T(128)}, bf16[16,8]{1,0:T(8,128)(2,1)S(1)}, bf16[16,8,64,128]{3,2,1,0:T(8,128)(2,1)}, /*index=5*/s32[]{:T(128)}, s32[]{:T(128)}) while((s32[]{:T(128)}, f32[8,64,128]{2,1,0:T(8,128)S(1)}, s32[]{:T(128)}, bf16[16,8]{1,0:T(8,128)(2,1)S(1)}, ...), condition=%wide.region_6.7_spmd.clone, body=%wide.region_5.6_spmd.clone.sunk | while | flops 327692 | bytes 655545 | solution.py:34
  175.7 2.1 multiply_add_fusion
  177.8 2.0 copy.39
  180.5 34.3 %psum.7 = f32[1024]{0:T(1024)S(1)} all-reduce(f32[1024]{0:T(1024)S(1)} %multiply_reduce_fusion), channel_id=1, replica_groups=mesh['seq'=16,'head'=16] {'head'}, use_global_device_ids=true, to_apply=%region_10.11 | all-reduce | flops 1024 | bytes 8192 | tf_op jit(solution)/shard_map/psum | solution.py:118
  214.8 9.5 %convolution_convert_fusion = bf16[1024,4096]{1,0:T(8,128)(2,1)} fusion(bf16[512,4096]{1,0:T(8,128)(2,1)} %param.25, f32[512]{0:T(512)S(1)} %copy-done.5, f32[1024]{0:T(1024)S(1)} %add_rsqrt_fusion, f32[1024,512]{1,0:T(8,128)S(1)} %copy.39, bf16[1024,512]{1,0:T(8,128)(2,1)S(1)} %copy-done.3), kind=kOutput, calls=%fused_computation.51 | convolution fusion | flops 4303880192 | bytes 15734784 | tf_op jit(solution)/shard_map/dot_general | solution.py:123
  224.3 90.8 %reduce-scatter.2.cloned.1.call-done = bf16[64,4096]{1,0:T(8,128)(2,1)} async-done(((bf16[1024,4096]{1,0:T(8,128)(2,1)}), bf16[64,4096]{1,0:T(8,128)(2,1)}) %reduce-scatter.2.cloned.1.call-update) | async-done | bytes 524304 | tf_op jit(solution)/shard_map/reduce_scatter | solution.py:122
  (139 shorter events, 53.6 us)
Async XLA Ops:
  6.5 12.1 %copy-start.2 = (bf16[1024,512]{1,0:T(8,128)(2,1)S(1)}, bf16[1024,512]{1,0:T(8,128)(2,1)}, u32[]{:S(2)}) copy-start(bf16[1024,512]{1,0:T(8,128)(2,1)} %param.15) | copy-start | bytes 3145732
  6.5 150.7 %all-gather.4.cloned.1.call-start = ((), (), s32[]{:S(2)}) async-start(), calls=%async_computation.2 | async-start | bytes 2228224 | tf_op jit(solution)/shard_map/all_gather | solution.py:21
  8.7 11.6 %collective-permute-start.1 = (bf16[3,256]{1,0:T(4,128)(2,1)S(1)}, bf16[3,256]{1,0:T(4,128)(2,1)S(1)}, u32[]{:S(2)}, u32[]{:S(2)}) collective-permute-start(bf16[3,256]{1,0:T(4,128)(2,1)S(1)} %slice.98), channel_id=1, source_target_pairs={{0,16},{16,32},{32,48},{48,64},{64,80},{80,96},{96,112},{112,128},... | collective-permute-start | bytes 4616 | tf_op jit(solution)/shard_map/ppermute | solution.py:15
  11.1 10.6 %collective-permute-start = (bf16[3,512]{1,0:T(4,128)(2,1)S(1)}, bf16[3,512]{1,0:T(4,128)(2,1)S(1)}, u32[]{:S(2)}, u32[]{:S(2)}) collective-permute-start(bf16[3,512]{1,0:T(4,128)(2,1)S(1)} %slice.70), channel_id=1, source_target_pairs={{0,16},{16,32},{32,48},{48,64},{64,80},{80,96},{96,112},{112,128},... | collective-permute-start | bytes 9224 | tf_op jit(solution)/shard_map/ppermute | solution.py:15
  20.3 1.6 copy-start
  29.3 86.5 %copy-start.6 = (u32[256]{0:T(256)S(1)}, u32[256]{0:T(256)}, u32[]{:S(2)}) copy-start(u32[256]{0:T(256)} %constant.75) | copy-start | bytes 3076
  115.7 199.3 %reduce-scatter.2.cloned.1.call-start = ((), (), s32[]{:S(2)}) async-start(), calls=%async_computation.1 | async-start | bytes 8912896 | tf_op jit(solution)/shard_map/reduce_scatter | solution.py:122
  174.1 1.6 copy-start.1
  174.1 1.6 copy-start.4
  177.8 2.0 copy-start.3
  179.8 35.0 %copy-start.5 = (f32[512]{0:T(512)S(1)}, f32[512]{0:T(512)}, u32[]{:S(2)}) copy-start(f32[512]{0:T(512)} %param.24) | copy-start | bytes 6148
Sparse Core Ops, SparseCore 0:
  115.8 41.3 all-gather.3
  224.4 90.5 reduce-scatter.1
where the time goes:
time: 324 us; the launch traced here: 322 us
  waiting for transfers between devices  97.5 us (30%)
  local copies, waits for them, and re-layouts  72.5 us (22%)
  blocking collectives  60.3 us (19%)
  matrix products  39.8 us (12%)
  other arithmetic  30.9 us (10%)
  between operations  14.3 us (4%)
  starting transfers between devices  5.88 us (2%)
    reduce_scatter x1, waiting for transfers between devices, local(): lax.psum_scatter(jnp.dot(normed, w_out, preferred_element_type=jnp.float3...  90.8 us
    dynamic_update_slice x8, local copies, waits for them, and re-layouts, local(): lax.scan(span_step, start, (split_blocks(x_heads), split_blocks(b_conv),...  51.4 us
    psum x1, blocking collectives, local(): squares = lax.psum(jnp.sum(gated * gated, axis=1), 'head')  34.3 us
    unnamed x1, blocking collectives  26.1 us
    select_n x16, other arithmetic, turn(): return jax.tree.map(lambda a, b: jnp.where(reached, a, b), new, before)  16.2 us
    dot_general x4, matrix products, span_step(): jnp.einsum('ijh,jhp->ihp', mixing, x_part, precision=lax.Precision.HIGHEST)  14.2 us
    dot_general x1, matrix products, local(): jnp.dot(normed, w_out, preferred_element_type=jnp.float32)  9.45 us
    all_gather x1, waiting for transfers between devices, carried_in(): lax.all_gather(part.astype(kind), axis)  6.71 us
  transfers between devices with their start and end apart: 4, of which 2 were waited for; matrix products, arithmetic and copies ran while one was open for 5% of the time, Pallas kernels for 0%

commit v1 on v0

--- a/solution.py
+++ b/solution.py
@@ -115,7 +115,9 @@
     )
     ssd = outputs.reshape(n_rows, head_count, HEAD_DIM) + carried + d_skip[None, :, None] * x_heads
     gated = ssd.reshape(n_rows, head_count * HEAD_DIM) * jax.nn.silu(z_gate.astype(jnp.float32))
-    squares = lax.psum(jnp.sum(gated * gated, axis=1), "head")
+    part_2 = jnp.sum(gated * gated, axis=1)
+    shards = lax.all_gather(part_2, "head")
+    squares = jnp.sum(shards, axis=0)
     normed = (gated * lax.rsqrt(squares / INNER + norm_eps)[:, None] * norm_gain[None, :]).astype(
         jnp.bfloat16
     )

time: 324 us -> 313 us (0.966)
  blocking collectives: 60.3 us -> 49.7 us
    psum x1 -> x0, blocking collectives: 34.3 us -> none  [local(): squares = lax.psum(jnp.sum(gated * gated, axis=1), 'head')]
    all_gather x0 -> x1, blocking collectives: none -> 23.6 us  [local(): shards = lax.all_gather(part_2, 'head')]
    unnamed x20 -> x18, local copies, waits for them, and re-layouts: 6.53 us -> 6.53 us
where the time goes in v1:
time: 313 us; the launch traced here: 310 us
  waiting for transfers between devices  94.3 us (30%)
  local copies, waits for them, and re-layouts  72.4 us (23%)
  blocking collectives  49.7 us (16%)
  matrix products  41 us (13%)
  other arithmetic  32.1 us (10%)
  between operations  14.3 us (5%)
  starting transfers between devices  5.88 us (2%)
    reduce_scatter x1, waiting for transfers between devices, local(): lax.psum_scatter(jnp.dot(normed, w_out, preferred_element_type=jnp.float3...  87.6 us
    dynamic_update_slice x8, local copies, waits for them, and re-layouts, local(): lax.scan(span_step, start, (split_blocks(x_heads), split_blocks(b_conv),...  51.4 us
    unnamed x1, blocking collectives  26.1 us
    all_gather x1, blocking collectives, local(): shards = lax.all_gather(part_2, 'head')  23.6 us
    select_n x16, other arithmetic, turn(): return jax.tree.map(lambda a, b: jnp.where(reached, a, b), new, before)  16.2 us
    dot_general x4, matrix products, span_step(): jnp.einsum('ijh,jhp->ihp', mixing, x_part, precision=lax.Precision.HIGHEST)  14.2 us
    dot_general x1, matrix products, local(): jnp.dot(normed, w_out, preferred_element_type=jnp.float32)  10.7 us
    all_gather x1, waiting for transfers between devices, carried_in(): lax.all_gather(part.astype(kind), axis)  6.71 us
  transfers between devices with their start and end apart: 4, of which 2 were waited for; matrix products, arithmetic and copies ran while one was open for 5% of the time, Pallas kernels for 0%

profile of v1, /device:TPU:2, one launch (start us, length us, event | category | flops | bytes accessed | tf_op | source)
XLA Modules:
  0.0 310.4 jit_solution(18087415153896727078)
XLA Ops:
  11.1 4.1 %collective-permute-start = (bf16[3,512]{1,0:T(4,128)(2,1)S(1)}, bf16[3,512]{1,0:T(4,128)(2,1)S(1)}, u32[]{:S(2)}, u32[]{:S(2)}) collective-permute-start(bf16[3,512]{1,0:T(4,128)(2,1)S(1)} %slice.70), channel_id=1, source_target_pairs={{0,16},{16,32},{32,48},{48,64},{64,80},{80,96},{96,112},{112,128},... | collective-permute-start | bytes 9224 | tf_op jit(solution)/shard_map/ppermute | solution.py:15
  23.1 2.4 reshape.119
  25.5 3.8 %copy.41 = f32[4,256,8,64]{1,3,2,0:T(8,128)} copy(f32[4,256,8,64]{3,2,1,0:T(8,128)} %reshape.119) | data formatting | bytes 4194304
  29.3 85.7 %while.27 = (s32[]{:T(128)}, f32[8,64,128]{2,1,0:T(8,128)S(1)}, f32[4,256,8,64]{1,0,3,2:T(4,128)}, f32[4,256,8]{1,2,0:T(8,128)S(1)}, f32[4,256,8,64]{1,3,2,0:T(8...) while((s32[]{:T(128)}, f32[8,64,128]{2,1,0:T(8,128)S(1)}, ...), condition=%wide.region_3.4_spmd.clone, body=%wide.region_0.3_spmd.clone.sunk | while | flops 825167872 | bytes 6557484 | solution.py:91
  31.6 3.5 %fusion.99 = f32[256,8,64]{0,2,1:T(8,128)S(1)} fusion(f32[256,8]{0,1:T(8,128)S(1)} %get-tuple-element.346, f32[256,256]{1,0:T(8,128)S(1)} %fusion.98, f32[256,8]{0,1:T(8,128)S(1)} %get-tuple-element.344, pred[256,256]{1,0:T(8,128)(4,1)S(1)} %iota_compare_fusion.2, f32[4,256,8,64]{1,3,2,0:T(8,128)} %get-tuple-element.379, s32[]{:T(128)} %get-tuple-element.364), kind=kOutput, calls=%fused_computation.12.clone.1 | convolution fusion | flops 404750336 | bytes 1401344 | tf_op jit(solution)/shard_map/while/body/eval_jaxpr/ijh,jhp->ihp/dot_general | solution.py:57
  36.9 12.3 %dynamic_update_slice.6 = f32[4,256,8,64]{1,0,3,2:T(4,128)} dynamic-update-slice(f32[4,256,8,64]{1,0,3,2:T(4,128)} %get-tuple-element.366, f32[1,256,8,64]{1,0,3,2:T(1,128)S(1)} %copy.59, s32[]{:T(128)} %get-tuple-element.364, s32[]{:T(128)} %constant.63.clone.1..sunk, s32[]{:T(128)} %constant.63.clone.1..sunk, s32[]{:T(128)} %constant.63.clone.1..sunk) | dynamic-update-slice | bytes 1048580 | tf_op jit(solution)/shard_map/while/body/jit(dynamic_update_index_in_dim)/dynamic_update_slice | solution.py:91
  53.0 3.5 %fusion.99 = f32[256,8,64]{0,2,1:T(8,128)S(1)} fusion(f32[256,8]{0,1:T(8,128)S(1)} %get-tuple-element.346, f32[256,256]{1,0:T(8,128)S(1)} %fusion.98, f32[256,8]{0,1:T(8,128)S(1)} %get-tuple-element.344, pred[256,256]{1,0:T(8,128)(4,1)S(1)} %iota_compare_fusion.2, f32[4,256,8,64]{1,3,2,0:T(8,128)} %get-tuple-element.379, s32[]{:T(128)} %get-tuple-element.364), kind=kOutput, calls=%fused_computation.12.clone.1 | convolution fusion | flops 404750336 | bytes 1401344 | tf_op jit(solution)/shard_map/while/body/eval_jaxpr/ijh,jhp->ihp/dot_general | solution.py:57
  58.3 12.3 %dynamic_update_slice.6 = f32[4,256,8,64]{1,0,3,2:T(4,128)} dynamic-update-slice(f32[4,256,8,64]{1,0,3,2:T(4,128)} %get-tuple-element.366, f32[1,256,8,64]{1,0,3,2:T(1,128)S(1)} %copy.59, s32[]{:T(128)} %get-tuple-element.364, s32[]{:T(128)} %constant.63.clone.1..sunk, s32[]{:T(128)} %constant.63.clone.1..sunk, s32[]{:T(128)} %constant.63.clone.1..sunk) | dynamic-update-slice | bytes 1048580 | tf_op jit(solution)/shard_map/while/body/jit(dynamic_update_index_in_dim)/dynamic_update_slice | solution.py:91
  74.4 3.5 %fusion.99 = f32[256,8,64]{0,2,1:T(8,128)S(1)} fusion(f32[256,8]{0,1:T(8,128)S(1)} %get-tuple-element.346, f32[256,256]{1,0:T(8,128)S(1)} %fusion.98, f32[256,8]{0,1:T(8,128)S(1)} %get-tuple-element.344, pred[256,256]{1,0:T(8,128)(4,1)S(1)} %iota_compare_fusion.2, f32[4,256,8,64]{1,3,2,0:T(8,128)} %get-tuple-element.379, s32[]{:T(128)} %get-tuple-element.364), kind=kOutput, calls=%fused_computation.12.clone.1 | convolution fusion | flops 404750336 | bytes 1401344 | tf_op jit(solution)/shard_map/while/body/eval_jaxpr/ijh,jhp->ihp/dot_general | solution.py:57
  79.7 12.3 %dynamic_update_slice.6 = f32[4,256,8,64]{1,0,3,2:T(4,128)} dynamic-update-slice(f32[4,256,8,64]{1,0,3,2:T(4,128)} %get-tuple-element.366, f32[1,256,8,64]{1,0,3,2:T(1,128)S(1)} %copy.59, s32[]{:T(128)} %get-tuple-element.364, s32[]{:T(128)} %constant.63.clone.1..sunk, s32[]{:T(128)} %constant.63.clone.1..sunk, s32[]{:T(128)} %constant.63.clone.1..sunk) | dynamic-update-slice | bytes 1048580 | tf_op jit(solution)/shard_map/while/body/jit(dynamic_update_index_in_dim)/dynamic_update_slice | solution.py:91
  95.8 3.5 %fusion.99 = f32[256,8,64]{0,2,1:T(8,128)S(1)} fusion(f32[256,8]{0,1:T(8,128)S(1)} %get-tuple-element.346, f32[256,256]{1,0:T(8,128)S(1)} %fusion.98, f32[256,8]{0,1:T(8,128)S(1)} %get-tuple-element.344, pred[256,256]{1,0:T(8,128)(4,1)S(1)} %iota_compare_fusion.2, f32[4,256,8,64]{1,3,2,0:T(8,128)} %get-tuple-element.379, s32[]{:T(128)} %get-tuple-element.364), kind=kOutput, calls=%fused_computation.12.clone.1 | convolution fusion | flops 404750336 | bytes 1401344 | tf_op jit(solution)/shard_map/while/body/eval_jaxpr/ijh,jhp->ihp/dot_general | solution.py:57
  101.2 12.3 %dynamic_update_slice.6 = f32[4,256,8,64]{1,0,3,2:T(4,128)} dynamic-update-slice(f32[4,256,8,64]{1,0,3,2:T(4,128)} %get-tuple-element.366, f32[1,256,8,64]{1,0,3,2:T(1,128)S(1)} %copy.59, s32[]{:T(128)} %get-tuple-element.364, s32[]{:T(128)} %constant.63.clone.1..sunk, s32[]{:T(128)} %constant.63.clone.1..sunk, s32[]{:T(128)} %constant.63.clone.1..sunk) | dynamic-update-slice | bytes 1048580 | tf_op jit(solution)/shard_map/while/body/jit(dynamic_update_index_in_dim)/dynamic_update_slice | solution.py:91
  117.4 26.1 %all-reduce = bf16[128]{0:T(256)(128)(2,1)S(1)} all-reduce(bf16[128]{0:T(256)(128)(2,1)S(1)} %dynamic-update-slice), channel_id=2, replica_groups=mesh['seq'=16,'head'=16] {'seq'}, use_global_device_ids=true, to_apply=%add | all-reduce | flops 128 | bytes 512
  143.6 2.3 reduce-window.16
  146.3 1.8 copy.44
  148.1 2.4 reshape.99
  150.5 6.7 %all-gather.5.cloned.1.call-done = bf16[128,64,128]{2,1,0:T(8,128)(2,1)} async-done(((bf16[8,64,128]{2,1,0:T(8,128)(2,1)}), bf16[128,64,128]{2,1,0:T(8,128)(2,1)}) %all-gather.5.cloned.1.call-update) | async-done | bytes 2097168 | tf_op jit(solution)/shard_map/all_gather | solution.py:21
  157.2 16.9 %while.28 = (s32[]{:T(128)}, f32[8,64,128]{2,1,0:T(8,128)S(1)}, s32[]{:T(128)}, bf16[16,8]{1,0:T(8,128)(2,1)S(1)}, bf16[16,8,64,128]{3,2,1,0:T(8,128)(2,1)}, /*index=5*/s32[]{:T(128)}, s32[]{:T(128)}) while((s32[]{:T(128)}, f32[8,64,128]{2,1,0:T(8,128)S(1)}, s32[]{:T(128)}, bf16[16,8]{1,0:T(8,128)(2,1)S(1)}, ...), condition=%wide.region_6.7_spmd.clone, body=%wide.region_5.6_spmd.clone.sunk | while | flops 327692 | bytes 655545 | solution.py:34
  175.7 2.1 multiply_add_fusion
  177.8 1.9 copy.45
  179.7 2.0 multiply_reduce_fusion
  181.6 23.6 %all-gather.2 = f32[16384]{0:T(1024)S(1)} all-gather(f32[1024]{0:T(1024)S(1)} %multiply_reduce_fusion), channel_id=4, replica_groups=mesh['seq'=16,'head'=16] {'head'}, dimensions={0}, use_global_device_ids=true | all-gather | bytes 69632 | tf_op jit(solution)/shard_map/all_gather | solution.py:119
  205.3 10.7 %convolution_convert_fusion = bf16[1024,4096]{1,0:T(8,128)(2,1)} fusion(bf16[512,4096]{1,0:T(8,128)(2,1)} %param.25, f32[512]{0:T(512)S(1)} %copy-done.4, f32[1024]{0:T(1024)S(1)} %add_rsqrt_fusion, f32[1024,512]{1,0:T(8,128)S(1)} %copy.45, bf16[1024,512]{1,0:T(8,128)(2,1)} %param.16), kind=kOutput, calls=%fused_computation.51 | convolution fusion | flops 4303880192 | bytes 15734784 | tf_op jit(solution)/shard_map/dot_general | solution.py:125
  216.0 87.6 %reduce-scatter.2.cloned.1.call-done = bf16[64,4096]{1,0:T(8,128)(2,1)} async-done(((bf16[1024,4096]{1,0:T(8,128)(2,1)}), bf16[64,4096]{1,0:T(8,128)(2,1)}) %reduce-scatter.2.cloned.1.call-update) | async-done | bytes 524304 | tf_op jit(solution)/shard_map/reduce_scatter | solution.py:124
  (139 shorter events, 54.6 us)
Async XLA Ops:
  6.5 12.1 %copy-start.2 = (bf16[1024,512]{1,0:T(8,128)(2,1)S(1)}, bf16[1024,512]{1,0:T(8,128)(2,1)}, u32[]{:S(2)}) copy-start(bf16[1024,512]{1,0:T(8,128)(2,1)} %param.15) | copy-start | bytes 3145732
  6.5 150.7 %all-gather.5.cloned.1.call-start = ((), (), s32[]{:S(2)}) async-start(), calls=%async_computation.2 | async-start | bytes 2228224 | tf_op jit(solution)/shard_map/all_gather | solution.py:21
  8.7 11.6 %collective-permute-start.1 = (bf16[3,256]{1,0:T(4,128)(2,1)S(1)}, bf16[3,256]{1,0:T(4,128)(2,1)S(1)}, u32[]{:S(2)}, u32[]{:S(2)}) collective-permute-start(bf16[3,256]{1,0:T(4,128)(2,1)S(1)} %slice.98), channel_id=1, source_target_pairs={{0,16},{16,32},{32,48},{48,64},{64,80},{80,96},{96,112},{112,128},... | collective-permute-start | bytes 4616 | tf_op jit(solution)/shard_map/ppermute | solution.py:15
  11.1 10.6 %collective-permute-start = (bf16[3,512]{1,0:T(4,128)(2,1)S(1)}, bf16[3,512]{1,0:T(4,128)(2,1)S(1)}, u32[]{:S(2)}, u32[]{:S(2)}) collective-permute-start(bf16[3,512]{1,0:T(4,128)(2,1)S(1)} %slice.70), channel_id=1, source_target_pairs={{0,16},{16,32},{32,48},{48,64},{64,80},{80,96},{96,112},{112,128},... | collective-permute-start | bytes 9224 | tf_op jit(solution)/shard_map/ppermute | solution.py:15
  20.3 1.6 copy-start
  29.3 86.5 %copy-start.5 = (u32[256]{0:T(256)S(1)}, u32[256]{0:T(256)}, u32[]{:S(2)}) copy-start(u32[256]{0:T(256)} %constant.75) | copy-start | bytes 3076
  115.7 187.8 %reduce-scatter.2.cloned.1.call-start = ((), (), s32[]{:S(2)}) async-start(), calls=%async_computation.1 | async-start | bytes 8912896 | tf_op jit(solution)/shard_map/reduce_scatter | solution.py:124
  174.1 1.6 copy-start.1
  174.1 1.6 copy-start.3
  179.7 25.6 %copy-start.4 = (f32[512]{0:T(512)S(1)}, f32[512]{0:T(512)}, u32[]{:S(2)}) copy-start(f32[512]{0:T(512)} %param.24) | copy-start | bytes 6148
Sparse Core Ops, SparseCore 0:
  115.8 41.3 all-gather.4
  216.1 87.4 reduce-scatter.1
